TPU v7x, 32 devices: a whole 2x2x4 slice. The times are simulated.
32 devices in a mesh: section: 2 (over x), tile: 16 (over z, y, core).
Axes of the slice: x: 2, y: 2, z: 4, core: 2. Of those that a mesh axis runs over, the one named last changes fastest.
Arguments:
- features: bfloat16 [16, 12, 1024, 128], P('tile', 'section'), may hold values from -6 to 6
- conv_weight: bfloat16 [5, 5, 128, 128], replicated, may hold values from -0.109375 to 0.109375
- head_weight: bfloat16 [128, 16], replicated, may hold values from -0.5 to 0.5
- kernels: bfloat16 [128, 1024, 2048], P('tile'), may hold values from -0.015625 to 0.015625
- source_weights: float32 [8], replicated, may hold values from 0.3 to 3
Outputs:
- intensity: float32 [16, 12, 1024], P('tile', 'section')
All inputs are finite; a program needn't handle non-finite values.
Results may differ from a plain program's by a relative error of at most 0.0018.
Values may be sent and summed in bfloat16 or wider, within the bound.
A program may use at most 128 MiB of HBM per device.

v0:
```python
import jax
import jax.numpy as jnp
from jax import lax
from jax.sharding import PartitionSpec as P

ANG = 8


def padded_2(block, sides, width):
    for axis, dim in sides:
        count = lax.axis_size(axis)
        forward = [(i, i + 1) for i in range(count - 1)]
        backward = [(target, source) for source, target in forward]
        low = lax.ppermute(
            lax.slice_in_dim(block, block.shape[dim] - width, None, axis=dim), axis, forward
        )
        high = lax.ppermute(lax.slice_in_dim(block, 0, width, axis=dim), axis, backward)
        block = jnp.concatenate([low, block, high], axis=dim)
    return block


def on_device(features, conv_weight, head_weight, kernels, source_weights):
    tile_count = lax.axis_size("tile")
    groups = tile_count // ANG
    windows = features.shape[0]
    rows_dev = features.shape[1]
    pixels = features.shape[2]
    angle_index = lax.axis_index("tile") // groups
    angle_weight = lax.dynamic_index_in_dim(source_weights, angle_index, 0, keepdims=False)
    padded = padded_2(features, (("section", 1),), 4)
    preact = lax.conv_general_dilated(
        padded,
        conv_weight,
        (1, 1),
        ((0, 0), (4, 4)),
        rhs_dilation=(2, 2),
        dimension_numbers=("NHWC", "HWIO", "NHWC"),
        preferred_element_type=jnp.float32,
    )
    hidden = jax.nn.gelu(preact, approximate=True).astype(jnp.bfloat16)
    near_field = jnp.einsum(
        "nrwc,cd->dnrw", hidden, head_weight, preferred_element_type=jnp.float32
    ).astype(jnp.bfloat16)
    near_field = near_field.reshape(ANG, 2, windows * rows_dev, pixels)
    outgoing = jnp.repeat(near_field, groups, axis=0)
    product = jnp.einsum(
        "sprw,kwv->pksrv",
        lax.all_to_all(outgoing, "tile", split_axis=0, concat_axis=0, tiled=True),
        kernels,
        preferred_element_type=jnp.float32,
    )
    real_part = product[0, :, :, :, :pixels] - product[1, :, :, :, pixels:]
    imag_part = product[0, :, :, :, pixels:] + product[1, :, :, :, :pixels]
    partial_rows = angle_weight * jnp.sum(real_part * real_part + imag_part * imag_part, axis=0)
    returned = lax.all_to_all(
        partial_rows.astype(jnp.bfloat16), "tile", split_axis=0, concat_axis=0, tiled=True
    ).astype(partial_rows.dtype)
    return jnp.sum(returned, axis=0, keepdims=True)


def solution(mesh):
    in_specs = (P("tile", "section", None, None), P(), P(), P("tile", None, None), P())
    out_specs = P("tile", "section", None)
    return jax.shard_map(
        on_device, mesh=mesh, in_specs=in_specs, out_specs=out_specs, check_vma=False
    )
```

profile of v0, /device:TPU:0, one launch (start us, length us, event | category | flops | bytes accessed | tf_op | source)
XLA Modules:
  0.0 117.0 jit_solution(17676578255435578340)
XLA Ops:
  0.0 0.0 copy-start
  0.0 0.0 copy-start.2
  0.0 1.8 %fusion.36 = (bf16[1,4,1024,128]{3,2,1,0:T(8,128)(2,1)S(1)}, bf16[1,4,1024,128]{3,2,1,0:T(8,128)(2,1)S(1)}) fusion(bf16[1,6,1024,128]{3,2,1,0:T(8,128)(2,1)} %param.5), kind=kLoop, calls=%fused_computation.39 | loop fusion | bytes 4194304 | tf_op jit(solution)/shard_map/slice | solution.py:15
  1.8 1.3 %collective-permute-start.1 = (bf16[1,4,1024,128]{3,2,1,0:T(8,128)(2,1)S(1)}, bf16[1,4,1024,128]{3,2,1,0:T(8,128)(2,1)S(1)}, u32[]{:S(2)}, u32[]{:S(2)}) collective-permute-start(bf16[1,4,1024,128]{3,2,1,0:T(8,128)(2,1)S(1)} %get-tuple-element.6), channel_id=1, source_target_pairs={{16,0},{17,1},{18,2},{19,3},{20,4},{21,5},{22,6},{23,7},{24,8},{25... | collective-permute-start | bytes 3145736 | tf_op jit(solution)/shard_map/ppermute | solution.py:17
  3.1 5.0 %collective-permute-start = (bf16[1,4,1024,128]{3,2,1,0:T(8,128)(2,1)S(1)}, bf16[1,4,1024,128]{3,2,1,0:T(8,128)(2,1)S(1)}, u32[]{:S(2)}, u32[]{:S(2)}) collective-permute-start(bf16[1,4,1024,128]{3,2,1,0:T(8,128)(2,1)S(1)} %get-tuple-element.5), channel_id=1, source_target_pairs={{0,16},{1,17},{2,18},{3,19},{4,20},{5,21},{6,22},{7,23},{8,24},{9,... | collective-permute-start | bytes 3145736 | tf_op jit(solution)/shard_map/ppermute | solution.py:14
  8.2 21.1 %collective-permute-done.1 = bf16[1,4,1024,128]{3,2,1,0:T(8,128)(2,1)S(1)} collective-permute-done((bf16[1,4,1024,128]{3,2,1,0:T(8,128)(2,1)S(1)}, bf16[1,4,1024,128]{3,2,1,0:T(8,128)(2,1)S(1)}, u32[]{:S(2)}, u32[]{:S(2)}) %collective-permute-start.1) | collective-permute-done | bytes 1048608 | tf_op jit(solution)/shard_map/ppermute | solution.py:17
  29.3 1.2 %collective-permute-done = bf16[1,4,1024,128]{3,2,1,0:T(8,128)(2,1)S(1)} collective-permute-done((bf16[1,4,1024,128]{3,2,1,0:T(8,128)(2,1)S(1)}, bf16[1,4,1024,128]{3,2,1,0:T(8,128)(2,1)S(1)}, u32[]{:S(2)}, u32[]{:S(2)}) %collective-permute-start) | collective-permute-done | bytes 1048608 | tf_op jit(solution)/shard_map/ppermute | solution.py:14
  30.5 0.0 copy-done.2
  30.5 0.4 maximum_bitcast_fusion
  31.0 2.8 %pad = bf16[14,1,1032,128]{3,2,0,1:T(8,128)(2,1)} pad(bf16[14,1,1024,128]{3,2,0,1:T(8,128)(2,1)S(1)} %maximum_bitcast_fusion, bf16[]{:T(256)} %constant.35), padding=0_0x0_0x4_4x0_0 | pad | bytes 7368706 | tf_op jit(solution)/shard_map/concatenate | solution.py:18
  33.8 6.5 %reshape.22 = bf16[14,1,8,129,128]{4,3,2,0,1:T(8,128)(2,1)} reshape(bf16[14,1,1032,128]{3,2,0,1:T(8,128)(2,1)} %pad) | data formatting | bytes 7397376 | tf_op jit(solution)/shard_map/conv_general_dilated | solution.py:31
  40.3 0.0 copy-start.5
  40.3 2.6 %copy.17 = bf16[14,1,8,129,128]{4,2,3,0,1:T(8,128)(2,1)S(1)} copy(bf16[14,1,8,129,128]{4,3,2,0,1:T(8,128)(2,1)} %reshape.22) | data formatting | bytes 7397376 | tf_op jit(solution)/shard_map/conv_general_dilated | solution.py:31
  42.9 0.1 slice.26
  43.0 0.0 copy-done
  43.0 0.0 copy-done.5
  43.0 11.1 %fusion.20 = bf16[6,8,129,128]{3,1,2,0:T(8,128)(2,1)S(1)} fusion(bf16[5,5,128,128]{3,2,1,0:T(8,128)(2,1)S(1)} %copy-done, bf16[14,1,7,8,128]{4,2,3,0,1:T(8,128)(2,1)S(1)} %slice.26, bf16[14,1,8,129,128]{4,2,3,0,1:T(8,128)(2,1)S(1)} %copy.17, pred[8,129]{0,1:T(8,128)(4,1)S(1)} %copy-done.5), kind=kOutput, calls=%fused_computation.20 | convolution fusion | flops 5092196352 | bytes 6304776 | tf_op jit(solution)/shard_map/conv_general_dilated | solution.py:31
  54.2 0.0 copy-start.3
  54.2 0.4 copy.18
  54.6 0.0 copy-start.4
  54.6 1.9 %reshape.26 = bf16[6,1,1032,128]{3,2,0,1:T(8,128)(2,1)} reshape(bf16[6,8,129,128]{3,2,1,0:T(8,128)(2,1)S(1)} %copy.18) | data formatting | bytes 3170304 | tf_op jit(solution)/shard_map/convert_element_type | solution.py:40
  56.5 0.0 copy-done.3
  56.5 1.9 %fusion.30 = bf16[16,6,1024]{2,0,1:T(8,128)(2,1)S(1)} fusion(bf16[6,1,1032,128]{3,2,0,1:T(8,128)(2,1)} %reshape.26, bf16[128,16]{0,1:T(8,128)(2,1)S(1)} %copy-done.3), kind=kOutput, calls=%fused_computation.31 | convolution fusion | flops 25264128 | bytes 1773568 | tf_op jit(solution)/shard_map/nrwc,cd->dnrw/dot_general | solution.py:41
  58.4 0.1 reshape.18
  58.5 0.1 copy.19
  58.7 1.0 broadcast_in_dim.6
  59.7 6.8 %all-to-all-start = ((bf16[16,2,6,1024]{3,1,2,0:T(2,128)(2,1)}), bf16[16,2,6,1024]{3,1,2,0:T(2,128)(2,1)S(1)}, u32[]{:S(2)}, u32[]{:S(2)}) async-start(bf16[16,2,6,1024]{3,1,2,0:T(2,128)(2,1)} %bitcast.6), calls=%async_computation | async-start | bytes 786432 | tf_op jit(solution)/shard_map/all_to_all | solution.py:48
  66.4 0.0 copy-done.4
  66.5 0.6 dynamic_slice.4
  67.0 11.6 %all-to-all-done = bf16[16,2,6,1024]{3,1,2,0:T(2,128)(2,1)S(1)} async-done(((bf16[16,2,6,1024]{3,1,2,0:T(2,128)(2,1)}), bf16[16,2,6,1024]{3,1,2,0:T(2,128)(2,1)S(1)}, u32[]{:S(2)}, u32[]{:S(2)}) %all-to-all-start) | async-done | bytes 393248 | tf_op jit(solution)/shard_map/all_to_all | solution.py:48
  78.6 17.4 %fusion.3 = f32[2,8,16,6,2048]{4,2,1,3,0:T(8,128)} fusion(bf16[8,1024,2048]{2,1,0:T(8,128)(2,1)} %param.8, bf16[16,2,6,1024,1]{3,1,2,0,4:T(2,128)(2,1)S(1)} %bitcast.38), kind=kOutput, calls=%fused_computation.4 | convolution fusion | flops 6442450944 | bytes 46530560 | tf_op jit(solution)/shard_map/sprw,kwv->pksrv/dot_general | solution.py:46
  96.0 0.0 copy-start.1
  96.0 6.3 %fusion.23 = f32[16,6,1024]{2,0,1:T(8,128)S(1)} fusion(f32[2,8,16,6,2048]{4,2,1,3,0:T(8,128)} %fusion.3), kind=kLoop, calls=%fused_computation.24 | loop fusion | flops 4620288 | bytes 12976128 | tf_op jit(solution)/shard_map/reduce_sum | solution.py:54
  102.3 0.7 multiply_convert_fusion
  103.0 0.1 copy.21
  103.1 13.2 %all_to_all.10 = bf16[16,6,1024]{2,1,0:T(8,128)(2,1)S(1)} all-to-all(bf16[16,6,1024]{2,1,0:T(8,128)(2,1)S(1)} %copy.21), channel_id=1, replica_groups=mesh['section'=2,'tile'=16] {'tile'}, dimensions={0} | all-to-all | bytes 393216 | tf_op jit(solution)/shard_map/all_to_all | solution.py:55
  116.3 0.1 convert_reduce_fusion
  116.4 0.6 broadcast_in_dim.7
  117.0 0.0 copy-done.1
Async XLA Ops:
  0.0 43.0 %copy-start = (bf16[5,5,128,128]{3,2,1,0:T(8,128)(2,1)S(1)}, bf16[5,5,128,128]{3,2,1,0:T(8,128)(2,1)}, u32[]{:S(2)}) copy-start(bf16[5,5,128,128]{3,2,1,0:T(8,128)(2,1)} %param.6) | copy-start | bytes 2457604
  0.0 30.5 %copy-start.2 = (bf16[1,6,1024,128]{3,2,1,0:T(8,128)(2,1)S(1)}, bf16[1,6,1024,128]{3,2,1,0:T(8,128)(2,1)}, u32[]{:S(2)}) copy-start(bf16[1,6,1024,128]{3,2,1,0:T(8,128)(2,1)} %param.5) | copy-start | bytes 4718596
  1.8 27.5 %collective-permute-start.1 = (bf16[1,4,1024,128]{3,2,1,0:T(8,128)(2,1)S(1)}, bf16[1,4,1024,128]{3,2,1,0:T(8,128)(2,1)S(1)}, u32[]{:S(2)}, u32[]{:S(2)}) collective-permute-start(bf16[1,4,1024,128]{3,2,1,0:T(8,128)(2,1)S(1)} %get-tuple-element.6), channel_id=1, source_target_pairs={{16,0},{17,1},{18,2},{19,3},{20,4},{21,5},{22,6},{23,7},{24,8},{25... | collective-permute-start | bytes 3145736 | tf_op jit(solution)/shard_map/ppermute | solution.py:17
  3.1 27.4 %collective-permute-start = (bf16[1,4,1024,128]{3,2,1,0:T(8,128)(2,1)S(1)}, bf16[1,4,1024,128]{3,2,1,0:T(8,128)(2,1)S(1)}, u32[]{:S(2)}, u32[]{:S(2)}) collective-permute-start(bf16[1,4,1024,128]{3,2,1,0:T(8,128)(2,1)S(1)} %get-tuple-element.5), channel_id=1, source_target_pairs={{0,16},{1,17},{2,18},{3,19},{4,20},{5,21},{6,22},{7,23},{8,24},{9,... | collective-permute-start | bytes 3145736 | tf_op jit(solution)/shard_map/ppermute | solution.py:14
  40.3 2.7 %copy-start.5 = (pred[8,129]{0,1:T(8,128)(4,1)S(1)}, pred[8,129]{0,1:T(8,128)(4,1)}, u32[]{:S(2)}) copy-start(pred[8,129]{0,1:T(8,128)(4,1)} %constant.39) | copy-start | bytes 3100
  54.2 2.4 %copy-start.3 = (bf16[128,16]{0,1:T(8,128)(2,1)S(1)}, bf16[128,16]{0,1:T(8,128)(2,1)}, u32[]{:S(2)}) copy-start(bf16[128,16]{0,1:T(8,128)(2,1)} %param.7) | copy-start | bytes 12292
  54.6 11.9 %copy-start.4 = (f32[8]{0:T(128)S(1)}, f32[8]{0:T(128)}, u32[]{:S(2)}) copy-start(f32[8]{0:T(128)} %param.9) | copy-start | bytes 100
  59.7 18.9 %all-to-all-start = ((bf16[16,2,6,1024]{3,1,2,0:T(2,128)(2,1)}), bf16[16,2,6,1024]{3,1,2,0:T(2,128)(2,1)S(1)}, u32[]{:S(2)}, u32[]{:S(2)}) async-start(bf16[16,2,6,1024]{3,1,2,0:T(2,128)(2,1)} %bitcast.6), calls=%async_computation | async-start | bytes 786432 | tf_op jit(solution)/shard_map/all_to_all | solution.py:48
  96.0 21.0 %copy-start.1 = (bf16[5,5,128,128]{3,2,1,0:T(8,128)(2,1)S(1)}, bf16[5,5,128,128]{3,2,1,0:T(8,128)(2,1)}, u32[]{:S(2)}) copy-start(bf16[5,5,128,128]{3,2,1,0:T(8,128)(2,1)} %param.6) | copy-start | bytes 2457604
where the time goes:
time: 117 us
  waiting for transfers between devices  33.9 us (29%)
  matrix products  30.4 us (26%)
  local copies, waits for them, and re-layouts  18.7 us (16%)
  blocking collectives  13.2 us (11%)
  starting transfers between devices  13.1 us (11%)
  other arithmetic  7.48 us (6%)
    ppermute x1, waiting for transfers between devices, padded_2(): lax.ppermute(lax.slice_in_dim(block, 0, width, axis=dim), axis, backward)  21.1 us
    dot_general x1, matrix products, on_device(): jnp.einsum('sprw,kwv->pksrv', lax.all_to_all(outgoing, 'tile', split_axis...  17.4 us
    all_to_all x1, blocking collectives, on_device(): lax.all_to_all(partial_rows.astype(jnp.bfloat16), 'tile', split_axis=0, c...  13.2 us
    all_to_all x1, waiting for transfers between devices, on_device(): lax.all_to_all(outgoing, 'tile', split_axis=0, concat_axis=0, tiled=True)  11.6 us
    conv_general_dilated x1, matrix products, on_device(): lax.conv_general_dilated(padded, conv_weight, (1, 1), ((0, 0), (4, 4)), r...  11.1 us
    conv_general_dilated x3, local copies, waits for them, and re-layouts, on_device(): lax.conv_general_dilated(padded, conv_weight, (1, 1), ((0, 0), (4, 4)), r...  9.17 us
    all_to_all x1, starting transfers between devices, on_device(): lax.all_to_all(outgoing, 'tile', split_axis=0, concat_axis=0, tiled=True)  6.76 us
    reduce_sum x1, other arithmetic, on_device(): jnp.sum(real_part * real_part + imag_part * imag_part, axis=0)  6.31 us
  transfers between devices with their start and end apart: 3, of which 3 were waited for; matrix products, arithmetic and copies ran while one was open for 1% of the time, Pallas kernels for 0%

commit v1 on v0

v1 whole, which is shorter than its diff:
```python
import functools

import jax
import jax.numpy as jnp
from jax import lax
from jax.experimental import pallas as pl
from jax.experimental.pallas import tpu as pltpu
from jax.sharding import PartitionSpec as P

ANG = 8
TAPS = 5
CHUNKS = 4
PAD = 16
BUNCH = 4
MESH = pl.DeviceIdType.MESH


def kernel(tiles, groups, feat, conv_w, head_t, operators, source_w, out_ref,
           x_ref, w_ref, l_ref, ns_ref, nr_ref, ef_ref, e_ref, g_ref, s_ref, r_ref, rr_ref,
           own_sem, w_sem, g_sem, halo_send, halo_recv, near_send, near_recv, near_own,
           ret_send, ret_recv, ret_own):
    sec = lax.axis_index("section")
    me = lax.axis_index("tile")
    half, pixels, chans = feat.shape[0], feat.shape[2], feat.shape[3]
    units = 2 * half
    pairs = units // 2
    kers = operators.shape[0]
    cw = pixels // CHUNKS
    span = TAPS * 2 * chans
    wide = 2 * chans

    own = pltpu.make_async_copy(
        feat.at[:, sec], x_ref.at[pl.ds(sec * half, half), pl.ds(PAD, pixels), :], own_sem)
    own.start()
    w_copies = []
    for d in range(3):
        for si in range(2):
            for so in range(2):
                tap = 2 * d + si - so
                if 0 <= tap < TAPS:
                    copy = pltpu.make_async_copy(
                        conv_w.at[tap],
                        w_ref.at[d, :, pl.ds(si * chans, chans), pl.ds(so * chans, chans)],
                        w_sem.at[len(w_copies)])
                    copy.start()
                    w_copies.append(copy)
                else:
                    w_ref[d, :, si * chans:(si + 1) * chans, so * chans:(so + 1) * chans] = jnp.zeros(
                        (TAPS, chans, chans), w_ref.dtype)

    barrier = pltpu.get_barrier_semaphore()

    def greet(i, carry):
        peer = lax.rem(me + i, tiles)
        pl.semaphore_signal(barrier, inc=1, device_id=(sec, peer), device_id_type=MESH)
        pl.semaphore_signal(barrier, inc=1, device_id=(1 - sec, peer), device_id_type=MESH)
        return carry

    pl.semaphore_signal(barrier, inc=1, device_id=(1 - sec, me), device_id_type=MESH)
    lax.fori_loop(1, tiles, greet, 0)
    pl.semaphore_wait(barrier, 2 * tiles - 1)

    halos = []
    for c in range(CHUNKS):
        lo = 0 if c == 0 else c * cw + PAD
        hi = pixels if c == CHUNKS - 1 else (c + 1) * cw + PAD
        copy = pltpu.make_async_remote_copy(
            src_ref=feat.at[:, 1 - sec, pl.ds(lo, hi - lo), :],
            dst_ref=x_ref.at[pl.ds(sec * half, half), pl.ds(PAD + lo, hi - lo), :],
            send_sem=halo_send.at[c], recv_sem=halo_recv.at[c],
            device_id=(1 - sec, me), device_id_type=MESH)
        copy.start()
        halos.append(copy)

    g_copies = []
    for k in range(kers):
        copy = pltpu.make_async_copy(operators.at[k], g_ref.at[k], g_sem.at[k])
        copy.start()
        g_copies.append(copy)

    edge = jnp.zeros((units, PAD, chans), x_ref.dtype)
    x_ref[:, 0:PAD, :] = edge
    x_ref[:, PAD + pixels:, :] = edge
    own.wait()
    for copy in w_copies:
        copy.wait()

    def near_copy(c, peer):
        return pltpu.make_async_remote_copy(
            src_ref=ns_ref.at[c, peer // groups], dst_ref=nr_ref.at[c, me],
            send_sem=near_send.at[c, peer], recv_sem=near_recv.at[c, me],
            device_id=(sec, peer), device_id_type=MESH)

    def near_arrival(c, peer):
        return pltpu.make_async_remote_copy(
            src_ref=ns_ref.at[c, 0], dst_ref=nr_ref.at[c, peer],
            send_sem=near_send.at[c, peer], recv_sem=near_recv.at[c, peer],
            device_id=(sec, peer), device_id_type=MESH)

    def conv_chunk(c, carry):
        for cc in range(CHUNKS):
            @pl.when(c == cc)
            def _():
                halos[cc].wait_recv()
        base = pl.multiple_of(c * cw, cw)
        for u in range(units):
            window = x_ref[u, pl.ds(base, cw + 2 * PAD), :]
            for j in range(TAPS):
                first = PAD + 2 * j - (TAPS - 1)
                at = (u // 2) * span + j * wide + (u % 2) * chans
                l_ref[:, at:at + chans] = window[first:first + cw, :]
        for p in range(pairs):
            d0, d1 = max(p - 1, 0), min(p + 1, pairs - 1)
            w0, w1 = d0 - p + 1, d1 - p + 2
            pre = jnp.dot(
                l_ref[:, d0 * span:(d1 + 1) * span],
                w_ref[w0:w1].reshape((w1 - w0) * span, wide),
                preferred_element_type=jnp.float32)
            hidden = jax.nn.gelu(pre, approximate=True).astype(jnp.bfloat16)
            for q in range(2):
                near = lax.dot_general(
                    head_t[...], hidden[:, q * chans:(q + 1) * chans],
                    (((1,), (1,)), ((), ())), preferred_element_type=jnp.float32)
                near = near.astype(jnp.bfloat16)
                for a in range(ANG):
                    ns_ref[c, a, 2 * p + q] = near[2 * a:2 * a + 2, :]

        def send(i, inner):
            near_copy(c, lax.rem(me + i, tiles)).start()
            return inner

        lax.fori_loop(1, tiles, send, 0)
        pltpu.make_async_copy(
            ns_ref.at[c, me // groups], nr_ref.at[c, me], near_own.at[c]).start()
        return carry

    lax.fori_loop(0, CHUNKS, conv_chunk, 0)

    for c in range(CHUNKS):
        pltpu.make_async_copy(
            ns_ref.at[c, me // groups], nr_ref.at[c, me], near_own.at[c]).wait()

        def arrive(i, carry):
            near_arrival(c, lax.rem(me + i, tiles)).wait_recv()
            return carry

        lax.fori_loop(1, tiles, arrive, 0)

        def place(t, carry):
            for i in range(BUNCH):
                for u in range(units):
                    at = i * units + u
                    pair = nr_ref[c, t * BUNCH + i, u].astype(jnp.float32)
                    ef_ref[0, t, at:at + 1, c * cw:(c + 1) * cw] = pair[0:1]
                    ef_ref[1, t, at:at + 1, c * cw:(c + 1) * cw] = pair[1:2]
            return carry

        lax.fori_loop(0, tiles // BUNCH, place, 0)
    rows = tiles * units
    real = ef_ref[0].reshape(rows, pixels).astype(jnp.bfloat16)
    imag = ef_ref[1].reshape(rows, pixels).astype(jnp.bfloat16)
    e_ref[0, 0:rows, :] = real
    e_ref[0, rows:, :] = imag
    e_ref[1, 0:rows, :] = -imag
    e_ref[1, rows:, :] = real

    weight = source_w[me // groups]
    for copy in g_copies:
        copy.wait()

    vw = 2 * chans

    def image(v, carry):
        at = pl.multiple_of(v * vw, vw)

        def one(k, inner):
            amp = jnp.dot(e_ref[0], g_ref[k, :, pl.ds(at, vw)], preferred_element_type=jnp.float32)
            amp += jnp.dot(e_ref[1], g_ref[k, :, pl.ds(pixels + at, vw)], preferred_element_type=jnp.float32)
            power = amp * amp
            s_ref[...] += power[0:rows] + power[rows:]
            return inner

        s_ref[...] = jnp.zeros_like(s_ref)
        lax.fori_loop(0, kers, one, 0)
        part = s_ref[...] * weight
        for t in range(tiles):
            for h in range(2):
                first = t * units + h * half
                r_ref[t, h, :, pl.ds(at, vw)] = part[first:first + half].astype(jnp.bfloat16)
        return carry

    lax.fori_loop(0, pixels // vw, image, 0)

    def ret_copy(h, peer):
        return pltpu.make_async_remote_copy(
            src_ref=r_ref.at[peer, h], dst_ref=rr_ref.at[sec, me],
            send_sem=ret_send.at[h, peer], recv_sem=ret_recv.at[sec, me],
            device_id=(h, peer), device_id_type=MESH)

    def ret_arrival(h, peer):
        return pltpu.make_async_remote_copy(
            src_ref=r_ref.at[peer, h], dst_ref=rr_ref.at[h, peer],
            send_sem=ret_send.at[h, peer], recv_sem=ret_recv.at[h, peer],
            device_id=(h, peer), device_id_type=MESH)

    def ret_go(i, carry):
        peer = lax.rem(me + i, tiles)
        ret_copy(sec, peer).start()
        ret_copy(1 - sec, peer).start()
        return carry

    ret_copy(1 - sec, me).start()
    lax.fori_loop(1, tiles, ret_go, 0)
    mine = pltpu.make_async_copy(r_ref.at[me, sec], rr_ref.at[sec, me], ret_own)
    mine.start()
    mine.wait()
    ret_arrival(1 - sec, me).wait()

    def ret_end(i, carry):
        peer = lax.rem(me + i, tiles)
        ret_arrival(sec, peer).wait()
        ret_arrival(1 - sec, peer).wait()
        return carry

    lax.fori_loop(1, tiles, ret_end, 0)

    for par in range(2):
        def gather(t, total):
            return total + rr_ref[par, t].astype(jnp.float32)

        total = lax.fori_loop(0, tiles, gather, jnp.zeros((half, pixels), jnp.float32))
        for j in range(half):
            out_ref[0, 2 * j + par:2 * j + par + 1, :] = total[j:j + 1]

    for copy in halos:
        copy.wait_send()
    for c in range(CHUNKS):
        def sent(i, carry):
            near_copy(c, lax.rem(me + i, tiles)).wait_send()
            return carry

        lax.fori_loop(1, tiles, sent, 0)


def on_device(features, conv_weight, head_weight, kernels, source_weights):
    tiles = lax.axis_size("tile")
    groups = tiles // ANG
    _, rows_dev, pixels, chans = features.shape
    half = rows_dev // 2
    units = 2 * half
    kers = kernels.shape[0]
    cw = pixels // CHUNKS
    bf16, f32 = jnp.bfloat16, jnp.float32
    feat = features.reshape(half, 2, pixels, chans)
    any_spec = pl.BlockSpec(memory_space=pl.ANY)
    return pl.pallas_call(
        functools.partial(kernel, tiles, groups),
        out_shape=jax.ShapeDtypeStruct((1, rows_dev, pixels), f32),
        in_specs=[
            any_spec,
            any_spec,
            pl.BlockSpec(memory_space=pltpu.VMEM),
            any_spec,
            pl.BlockSpec(memory_space=pltpu.SMEM),
        ],
        out_specs=pl.BlockSpec(memory_space=pltpu.VMEM),
        scratch_shapes=[
            pltpu.VMEM((units, pixels + 2 * PAD, chans), bf16),
            pltpu.VMEM((3, TAPS, 2 * chans, 2 * chans), bf16),
            pltpu.VMEM((cw, (units // 2) * TAPS * 2 * chans), bf16),
            pltpu.VMEM((CHUNKS, ANG, units, 2, cw), bf16),
            pltpu.VMEM((CHUNKS, tiles, units, 2, cw), bf16),
            pltpu.VMEM((2, tiles // BUNCH, BUNCH * units, pixels), f32),
            pltpu.VMEM((2, tiles * units * 2, pixels), bf16),
            pltpu.VMEM((kers, pixels, 2 * pixels), bf16),
            pltpu.VMEM((tiles * units, 2 * chans), f32),
            pltpu.VMEM((tiles, 2, half, pixels), bf16),
            pltpu.VMEM((2, tiles, half, pixels), bf16),
            pltpu.SemaphoreType.DMA,
            pltpu.SemaphoreType.DMA((10,)),
            pltpu.SemaphoreType.DMA((kers,)),
            pltpu.SemaphoreType.DMA((CHUNKS,)),
            pltpu.SemaphoreType.DMA((CHUNKS,)),
            pltpu.SemaphoreType.DMA((CHUNKS, tiles)),
            pltpu.SemaphoreType.DMA((CHUNKS, tiles)),
            pltpu.SemaphoreType.DMA((CHUNKS,)),
            pltpu.SemaphoreType.DMA((2, tiles)),
            pltpu.SemaphoreType.DMA((2, tiles)),
            pltpu.SemaphoreType.DMA,
        ],
        compiler_params=pltpu.CompilerParams(
            collective_id=0, has_side_effects=True, vmem_limit_bytes=66_000_000),
    )(feat, conv_weight, head_weight.T, kernels, source_weights)


def solution(mesh):
    in_specs = (P("tile", "section", None, None), P(), P(), P("tile", None, None), P())
    out_specs = P("tile", "section", None)
    return jax.shard_map(
        on_device, mesh=mesh, in_specs=in_specs, out_specs=out_specs, check_vma=False
    )
```

time: 117 us -> 58.7 us (0.50)
  Pallas kernels: 0 us -> 56.2 us
  waiting for transfers between devices: 33.9 us -> 0 us
  matrix products: 30.4 us -> 0 us
  local copies, waits for them, and re-layouts: 18.7 us -> 1.39 us
  blocking collectives: 13.2 us -> 0 us
  starting transfers between devices: 13.1 us -> 0 us
  other arithmetic: 7.48 us -> 0 us
    pallas_call x0 -> x1, Pallas kernels: none -> 56.2 us  [on_device(): pl.pallas_call(functools.partial(kernel, tiles, groups), out_shape=jax.Sh...]
    ppermute x2 -> x0, waiting for transfers between devices: 22.4 us -> none  [the longest x1 21.1 us: padded_2(): lax.ppermute(lax.slice_in_dim(block, 0, width, axis=dim), axis, backward)]
    dot_general x2 -> x0, matrix products: 19.3 us -> none  [the longest x1 17.4 us: on_device(): jnp.einsum('sprw,kwv->pksrv', lax.all_to_all(outgoing, 'tile', split_axis...]
    all_to_all x1 -> x0, blocking collectives: 13.2 us -> none  [on_device(): lax.all_to_all(partial_rows.astype(jnp.bfloat16), 'tile', split_axis=0, c...]
    all_to_all x1 -> x0, waiting for transfers between devices: 11.6 us -> none  [on_device(): lax.all_to_all(outgoing, 'tile', split_axis=0, concat_axis=0, tiled=True)]
    conv_general_dilated x1 -> x0, matrix products: 11.1 us -> none  [on_device(): lax.conv_general_dilated(padded, conv_weight, (1, 1), ((0, 0), (4, 4)), r...]
    conv_general_dilated x3 -> x0, local copies, waits for them, and re-layouts: 9.17 us -> none  [on_device(): lax.conv_general_dilated(padded, conv_weight, (1, 1), ((0, 0), (4, 4)), r...]
    all_to_all x1 -> x0, starting transfers between devices: 6.76 us -> none  [on_device(): lax.all_to_all(outgoing, 'tile', split_axis=0, concat_axis=0, tiled=True)]
  transfers between devices with their start and end apart: 3 -> 0, of which waited for: 3 -> 0; matrix products, arithmetic and copies ran while one was open for 1% -> 0% of each run, Pallas kernels for 0% -> 0%
where the time goes in v1:
time: 58.7 us; the launch traced here: 57.6 us
  Pallas kernels  56.2 us (96%)
  local copies, waits for them, and re-layouts  1.39 us (2%)
    pallas_call x1, Pallas kernels, on_device(): pl.pallas_call(functools.partial(kernel, tiles, groups), out_shape=jax.Sh...  56.2 us
    pallas_call x1, local copies, waits for them, and re-layouts, on_device(): pl.pallas_call(functools.partial(kernel, tiles, groups), out_shape=jax.Sh...  1.39 us

profile of v1, /device:TPU:0, one launch (start us, length us, event | category | flops | bytes accessed | tf_op | source)
XLA Modules:
  0.0 57.6 jit_solution(14863462087774241078)
XLA Ops:
  0.0 56.2 %shard_map.55 = f32[1,6,1024]{2,1,0:T(8,128)} custom-call(bf16[3,2,1024,128]{3,2,1,0:T(8,128)(2,1)} %bitcast.2, bf16[5,5,128,128]{3,2,1,0:T(8,128)(2,1)} %conv_w.1, bf16[16,128]{1,0:T(8,128)(2,1)} %bitcast.3, bf16[8,1024,2048]{2,1,0:T(8,128)(2,1)} %operators.1, f32[8]{0:T(128)} %source_w.1), custom_call_target="tpu_custom_call" | custom-call | tf_op jit(solution)/shard_map/pallas_call | solution.py:256
  56.2 1.4 %copy.6 = f32[1,6,1024]{2,0,1:T(1,128)} copy(f32[1,6,1024]{2,1,0:T(8,128)} %shard_map.55) | data formatting | bytes 49152 | tf_op jit(solution)/shard_map/pallas_call | solution.py:256

commit v2 on v1

--- a/solution.py
+++ b/solution.py
@@ -12,11 +12,12 @@
 CHUNKS = 4
 PAD = 16
 BUNCH = 4
+SENDS = 2
 MESH = pl.DeviceIdType.MESH
 
 
 def kernel(tiles, groups, feat, conv_w, head_t, operators, source_w, out_ref,
-           x_ref, w_ref, l_ref, ns_ref, nr_ref, ef_ref, e_ref, g_ref, s_ref, r_ref, rr_ref,
+           x_ref, w_ref, l_ref, ns_ref, nr_ref, ef_ref, e_ref, acc_ref, g_ref, s_ref, r_ref, rr_ref,
            own_sem, w_sem, g_sem, halo_send, halo_recv, near_send, near_recv, near_own,
            ret_send, ret_recv, ret_own):
     sec = lax.axis_index("section")
@@ -134,103 +135,137 @@
             ns_ref.at[c, me // groups], nr_ref.at[c, me], near_own.at[c]).start()
         return carry
 
-    lax.fori_loop(0, CHUNKS, conv_chunk, 0)
-
-    for c in range(CHUNKS):
+    rows = tiles * units
+    vw = 2 * chans
+    part_v = pixels // vw
+    per_send = part_v // SENDS
+    weight = source_w[me // groups]
+
+    def gather_chunk(c):
         pltpu.make_async_copy(
             ns_ref.at[c, me // groups], nr_ref.at[c, me], near_own.at[c]).wait()
 
-        def arrive(i, carry):
+        def arrive(i, inner):
             near_arrival(c, lax.rem(me + i, tiles)).wait_recv()
-            return carry
+            return inner
 
         lax.fori_loop(1, tiles, arrive, 0)
 
-        def place(t, carry):
+        def place(t, inner):
             for i in range(BUNCH):
                 for u in range(units):
                     at = i * units + u
                     pair = nr_ref[c, t * BUNCH + i, u].astype(jnp.float32)
-                    ef_ref[0, t, at:at + 1, c * cw:(c + 1) * cw] = pair[0:1]
-                    ef_ref[1, t, at:at + 1, c * cw:(c + 1) * cw] = pair[1:2]
-            return carry
+                    ef_ref[0, t, at:at + 1, :] = pair[0:1]
+                    ef_ref[1, t, at:at + 1, :] = pair[1:2]
+            return inner
 
         lax.fori_loop(0, tiles // BUNCH, place, 0)
-    rows = tiles * units
-    real = ef_ref[0].reshape(rows, pixels).astype(jnp.bfloat16)
-    imag = ef_ref[1].reshape(rows, pixels).astype(jnp.bfloat16)
-    e_ref[0, 0:rows, :] = real
-    e_ref[0, rows:, :] = imag
-    e_ref[1, 0:rows, :] = -imag
-    e_ref[1, rows:, :] = real
-
-    weight = source_w[me // groups]
-    for copy in g_copies:
-        copy.wait()
-
-    vw = 2 * chans
-
-    def image(v, carry):
+        real = ef_ref[0].reshape(rows, cw).astype(jnp.bfloat16)
+        imag = ef_ref[1].reshape(rows, cw).astype(jnp.bfloat16)
+        e_ref[0:rows, 0:cw] = real
+        e_ref[rows:, 0:cw] = imag
+        e_ref[0:rows, cw:] = -imag
+        e_ref[rows:, cw:] = real
+
+    def product(c, v, k):
+        top = pl.multiple_of(c * cw, cw)
         at = pl.multiple_of(v * vw, vw)
-
-        def one(k, inner):
-            amp = jnp.dot(e_ref[0], g_ref[k, :, pl.ds(at, vw)], preferred_element_type=jnp.float32)
-            amp += jnp.dot(e_ref[1], g_ref[k, :, pl.ds(pixels + at, vw)], preferred_element_type=jnp.float32)
-            power = amp * amp
-            s_ref[...] += power[0:rows] + power[rows:]
+        amp = jnp.dot(e_ref[:, 0:cw], g_ref[k, pl.ds(top, cw), pl.ds(at, vw)],
+                      preferred_element_type=jnp.float32)
+        return amp + jnp.dot(e_ref[:, cw:], g_ref[k, pl.ds(top, cw), pl.ds(pixels + at, vw)],
+                             preferred_element_type=jnp.float32)
+
+    def step(c, carry):
+        @pl.when(c < CHUNKS)
+        def _():
+            conv_chunk(c, 0)
+
+        @pl.when(c > 0)
+        def _():
+            gather_chunk(c - 1)
+
+            def image(k, inner):
+                @pl.when(c == 1)
+                def _():
+                    for kk in range(kers):
+                        @pl.when(k == kk)
+                        def _():
+                            g_copies[kk].wait()
+
+                for v in range(part_v):
+                    acc_ref[k, v] += product(c - 1, v, k)
+                return inner
+
+            lax.fori_loop(0, kers, image, 0)
+        return carry
+
+    acc_ref[...] = jnp.zeros_like(acc_ref)
+    lax.fori_loop(0, CHUNKS, step, 0)
+    gather_chunk(CHUNKS - 1)
+
+    def ret_copy(n, h, peer):
+        return pltpu.make_async_remote_copy(
+            src_ref=r_ref.at[n, peer, h], dst_ref=rr_ref.at[n, sec, me],
+            send_sem=ret_send.at[n, h, peer], recv_sem=ret_recv.at[n, sec, me],
+            device_id=(h, peer), device_id_type=MESH)
+
+    def ret_arrival(n, h, peer):
+        return pltpu.make_async_remote_copy(
+            src_ref=r_ref.at[n, peer, h], dst_ref=rr_ref.at[n, h, peer],
+            send_sem=ret_send.at[n, h, peer], recv_sem=ret_recv.at[n, h, peer],
+            device_id=(h, peer), device_id_type=MESH)
+
+    def ret_mine(n):
+        return pltpu.make_async_copy(r_ref.at[n, me, sec], rr_ref.at[n, sec, me], ret_own.at[n])
+
+    for n in range(SENDS):
+        def last(k, inner):
+            for m in range(per_send):
+                v = n * per_send + m
+                amp = acc_ref[k, v] + product(CHUNKS - 1, v, k)
+                power = amp * amp
+                s_ref[:, m * vw:(m + 1) * vw] += power[0:rows] + power[rows:]
             return inner
 
         s_ref[...] = jnp.zeros_like(s_ref)
-        lax.fori_loop(0, kers, one, 0)
+        lax.fori_loop(0, kers, last, 0)
         part = s_ref[...] * weight
         for t in range(tiles):
             for h in range(2):
                 first = t * units + h * half
-                r_ref[t, h, :, pl.ds(at, vw)] = part[first:first + half].astype(jnp.bfloat16)
-        return carry
-
-    lax.fori_loop(0, pixels // vw, image, 0)
-
-    def ret_copy(h, peer):
-        return pltpu.make_async_remote_copy(
-            src_ref=r_ref.at[peer, h], dst_ref=rr_ref.at[sec, me],
-            send_sem=ret_send.at[h, peer], recv_sem=ret_recv.at[sec, me],
-            device_id=(h, peer), device_id_type=MESH)
-
-    def ret_arrival(h, peer):
-        return pltpu.make_async_remote_copy(
-            src_ref=r_ref.at[peer, h], dst_ref=rr_ref.at[h, peer],
-            send_sem=ret_send.at[h, peer], recv_sem=ret_recv.at[h, peer],
-            device_id=(h, peer), device_id_type=MESH)
-
-    def ret_go(i, carry):
-        peer = lax.rem(me + i, tiles)
-        ret_copy(sec, peer).start()
-        ret_copy(1 - sec, peer).start()
-        return carry
-
-    ret_copy(1 - sec, me).start()
-    lax.fori_loop(1, tiles, ret_go, 0)
-    mine = pltpu.make_async_copy(r_ref.at[me, sec], rr_ref.at[sec, me], ret_own)
-    mine.start()
-    mine.wait()
-    ret_arrival(1 - sec, me).wait()
-
-    def ret_end(i, carry):
-        peer = lax.rem(me + i, tiles)
-        ret_arrival(sec, peer).wait()
-        ret_arrival(1 - sec, peer).wait()
-        return carry
-
-    lax.fori_loop(1, tiles, ret_end, 0)
-
-    for par in range(2):
-        def gather(t, total):
-            return total + rr_ref[par, t].astype(jnp.float32)
-
-        total = lax.fori_loop(0, tiles, gather, jnp.zeros((half, pixels), jnp.float32))
-        for j in range(half):
-            out_ref[0, 2 * j + par:2 * j + par + 1, :] = total[j:j + 1]
+                r_ref[n, t, h] = part[first:first + half].astype(jnp.bfloat16)
+
+        def ret_go(i, carry):
+            peer = lax.rem(me + i, tiles)
+            ret_copy(n, sec, peer).start()
+            ret_copy(n, 1 - sec, peer).start()
+            return carry
+
+        lax.fori_loop(1, tiles, ret_go, 0)
+        ret_copy(n, 1 - sec, me).start()
+        ret_mine(n).start()
+
+    for n in range(SENDS):
+        ret_mine(n).wait()
+        ret_arrival(n, 1 - sec, me).wait()
+
+        def ret_end(i, carry):
+            peer = lax.rem(me + i, tiles)
+            ret_arrival(n, sec, peer).wait()
+            ret_arrival(n, 1 - sec, peer).wait()
+            return carry
+
+        lax.fori_loop(1, tiles, ret_end, 0)
+
+        for par in range(2):
+            def gather(t, total):
+                return total + rr_ref[n, par, t].astype(jnp.float32)
+
+            total = lax.fori_loop(0, tiles, gather, jnp.zeros((half, pixels // SENDS), jnp.float32))
+            cols = slice(n * (pixels // SENDS), (n + 1) * (pixels // SENDS))
+            for j in range(half):
+                out_ref[0, 2 * j + par:2 * j + par + 1, cols] = total[j:j + 1]
 
     for copy in halos:
         copy.wait_send()
@@ -270,12 +305,13 @@
             pltpu.VMEM((cw, (units // 2) * TAPS * 2 * chans), bf16),
             pltpu.VMEM((CHUNKS, ANG, units, 2, cw), bf16),
             pltpu.VMEM((CHUNKS, tiles, units, 2, cw), bf16),
-            pltpu.VMEM((2, tiles // BUNCH, BUNCH * units, pixels), f32),
-            pltpu.VMEM((2, tiles * units * 2, pixels), bf16),
+            pltpu.VMEM((2, tiles // BUNCH, BUNCH * units, cw), f32),
+            pltpu.VMEM((tiles * units * 2, 2 * cw), bf16),
+            pltpu.VMEM((kers, pixels // (2 * chans), tiles * units * 2, 2 * chans), f32),
             pltpu.VMEM((kers, pixels, 2 * pixels), bf16),
-            pltpu.VMEM((tiles * units, 2 * chans), f32),
-            pltpu.VMEM((tiles, 2, half, pixels), bf16),
-            pltpu.VMEM((2, tiles, half, pixels), bf16),
+            pltpu.VMEM((tiles * units, pixels // SENDS), f32),
+            pltpu.VMEM((SENDS, tiles, 2, half, pixels // SENDS), bf16),
+            pltpu.VMEM((SENDS, 2, tiles, half, pixels // SENDS), bf16),
             pltpu.SemaphoreType.DMA,
             pltpu.SemaphoreType.DMA((10,)),
             pltpu.SemaphoreType.DMA((kers,)),
@@ -284,9 +320,9 @@
             pltpu.SemaphoreType.DMA((CHUNKS, tiles)),
             pltpu.SemaphoreType.DMA((CHUNKS, tiles)),
             pltpu.SemaphoreType.DMA((CHUNKS,)),
-            pltpu.SemaphoreType.DMA((2, tiles)),
-            pltpu.SemaphoreType.DMA((2, tiles)),
-            pltpu.SemaphoreType.DMA,
+            pltpu.SemaphoreType.DMA((SENDS, 2, tiles)),
+            pltpu.SemaphoreType.DMA((SENDS, 2, tiles)),
+            pltpu.SemaphoreType.DMA((SENDS,)),
         ],
         compiler_params=pltpu.CompilerParams(
             collective_id=0, has_side_effects=True, vmem_limit_bytes=66_000_000),

time: 58.7 us -> 56 us (0.954); the launches traced: 57.6 us -> 55.8 us
  Pallas kernels: 56.2 us -> 54.4 us
    pallas_call x1, Pallas kernels: 56.2 us -> 54.4 us  [on_device(): pl.pallas_call(functools.partial(kernel, tiles, groups), out_shape=jax.Sh...]
where the time goes in v2:
time: 56 us; the launch traced here: 55.8 us
  Pallas kernels  54.4 us (97%)
  local copies, waits for them, and re-layouts  1.39 us (2%)
    pallas_call x1, Pallas kernels, on_device(): pl.pallas_call(functools.partial(kernel, tiles, groups), out_shape=jax.Sh...  54.4 us
    pallas_call x1, local copies, waits for them, and re-layouts, on_device(): pl.pallas_call(functools.partial(kernel, tiles, groups), out_shape=jax.Sh...  1.39 us

profile of v2, /device:TPU:0, one launch (start us, length us, event | category | flops | bytes accessed | tf_op | source)
XLA Modules:
  0.0 55.8 jit_solution(14865487057795618303)
XLA Ops:
  0.0 54.4 %shard_map.55 = f32[1,6,1024]{2,1,0:T(8,128)} custom-call(bf16[3,2,1024,128]{3,2,1,0:T(8,128)(2,1)} %bitcast.2, bf16[5,5,128,128]{3,2,1,0:T(8,128)(2,1)} %conv_w.1, bf16[16,128]{1,0:T(8,128)(2,1)} %bitcast.3, bf16[8,1024,2048]{2,1,0:T(8,128)(2,1)} %operators.1, f32[8]{0:T(128)} %source_w.1), custom_call_target="tpu_custom_call" | custom-call | tf_op jit(solution)/shard_map/pallas_call | solution.py:291
  54.4 1.4 %copy.6 = f32[1,6,1024]{2,0,1:T(1,128)} copy(f32[1,6,1024]{2,1,0:T(8,128)} %shard_map.55) | data formatting | bytes 49152 | tf_op jit(solution)/shard_map/pallas_call | solution.py:291

commit v3 on v2

--- a/solution.py
+++ b/solution.py
@@ -104,13 +104,19 @@
             def _():
                 halos[cc].wait_recv()
         base = pl.multiple_of(c * cw, cw)
-        for u in range(units):
+        def build(u):
             window = x_ref[u, pl.ds(base, cw + 2 * PAD), :]
             for j in range(TAPS):
                 first = PAD + 2 * j - (TAPS - 1)
                 at = (u // 2) * span + j * wide + (u % 2) * chans
                 l_ref[:, at:at + chans] = window[first:first + cw, :]
+
+        build(0)
+        build(1)
         for p in range(pairs):
+            if p + 1 < pairs:
+                build(2 * p + 2)
+                build(2 * p + 3)
             d0, d1 = max(p - 1, 0), min(p + 1, pairs - 1)
             w0, w1 = d0 - p + 1, d1 - p + 2
             pre = jnp.dot(
@@ -139,6 +145,7 @@
     vw = 2 * chans
     part_v = pixels // vw
     per_send = part_v // SENDS
+    unroll = 4 if kers % 4 == 0 else 1
     weight = source_w[me // groups]
 
     def gather_chunk(c):
@@ -185,19 +192,18 @@
         def _():
             gather_chunk(c - 1)
 
-            def image(k, inner):
-                @pl.when(c == 1)
-                def _():
-                    for kk in range(kers):
-                        @pl.when(k == kk)
-                        def _():
-                            g_copies[kk].wait()
-
-                for v in range(part_v):
-                    acc_ref[k, v] += product(c - 1, v, k)
+            @pl.when(c == 1)
+            def _():
+                for copy in g_copies:
+                    copy.wait()
+
+            def image(kb, inner):
+                for i in range(unroll):
+                    for v in range(part_v):
+                        acc_ref[kb * unroll + i, v] += product(c - 1, v, kb * unroll + i)
                 return inner
 
-            lax.fori_loop(0, kers, image, 0)
+            lax.fori_loop(0, kers // unroll, image, 0)
         return carry
 
     acc_ref[...] = jnp.zeros_like(acc_ref)
@@ -220,16 +226,18 @@
         return pltpu.make_async_copy(r_ref.at[n, me, sec], rr_ref.at[n, sec, me], ret_own.at[n])
 
     for n in range(SENDS):
-        def last(k, inner):
-            for m in range(per_send):
-                v = n * per_send + m
-                amp = acc_ref[k, v] + product(CHUNKS - 1, v, k)
-                power = amp * amp
-                s_ref[:, m * vw:(m + 1) * vw] += power[0:rows] + power[rows:]
+        def last(kb, inner):
+            for i in range(unroll):
+                k = kb * unroll + i
+                for m in range(per_send):
+                    v = n * per_send + m
+                    amp = acc_ref[k, v] + product(CHUNKS - 1, v, k)
+                    power = amp * amp
+                    s_ref[:, m * vw:(m + 1) * vw] += power[0:rows] + power[rows:]
             return inner
 
         s_ref[...] = jnp.zeros_like(s_ref)
-        lax.fori_loop(0, kers, last, 0)
+        lax.fori_loop(0, kers // unroll, last, 0)
         part = s_ref[...] * weight
         for t in range(tiles):
             for h in range(2):

time: 56 us -> 52.7 us (0.941)
  Pallas kernels: 54.4 us -> 51.1 us
    pallas_call x1, Pallas kernels: 54.4 us -> 51.1 us  [on_device(): pl.pallas_call(functools.partial(kernel, tiles, groups), out_shape=jax.Sh...]
where the time goes in v3:
time: 52.7 us; the launch traced here: 52.5 us
  Pallas kernels  51.1 us (97%)
  local copies, waits for them, and re-layouts  1.39 us (3%)
    pallas_call x1, Pallas kernels, on_device(): pl.pallas_call(functools.partial(kernel, tiles, groups), out_shape=jax.Sh...  51.1 us
    pallas_call x1, local copies, waits for them, and re-layouts, on_device(): pl.pallas_call(functools.partial(kernel, tiles, groups), out_shape=jax.Sh...  1.39 us

profile of v3, /device:TPU:0, one launch (start us, length us, event | category | flops | bytes accessed | tf_op | source)
XLA Modules:
  0.0 52.5 jit_solution(5545985762620052203)
XLA Ops:
  0.0 51.1 %shard_map.55 = f32[1,6,1024]{2,1,0:T(8,128)} custom-call(bf16[3,2,1024,128]{3,2,1,0:T(8,128)(2,1)} %bitcast.2, bf16[5,5,128,128]{3,2,1,0:T(8,128)(2,1)} %conv_w.1, bf16[16,128]{1,0:T(8,128)(2,1)} %bitcast.3, bf16[8,1024,2048]{2,1,0:T(8,128)(2,1)} %operators.1, f32[8]{0:T(128)} %source_w.1), custom_call_target="tpu_custom_call" | custom-call | tf_op jit(solution)/shard_map/pallas_call | solution.py:299
  51.1 1.4 %copy.6 = f32[1,6,1024]{2,0,1:T(1,128)} copy(f32[1,6,1024]{2,1,0:T(8,128)} %shard_map.55) | data formatting | bytes 49152 | tf_op jit(solution)/shard_map/pallas_call | solution.py:299
